TPU v7x, 256 devices: a whole 4x4x8 slice. The times are simulated.
256 devices in a mesh: br: 64 (over z, y_hi, x), bus: 4 (over y_lo, core).
Axes of the slice: x: 4, y: 4 (y_hi: 2, y_lo: 2; y = y_hi * 2 + y_lo), z: 8, core: 2. Of those that a mesh axis runs over, the one named last changes fastest.
Arguments:
- net_load: bfloat16 [128, 60416], P('br', 'bus'), may hold values from -6 to 6
- release: float32 [128, 1024], P('br'), may hold values from 0 to 2
- plant_bus: int32 [1024], replicated, may hold values from 0 to 60415
- efficiency: float32 [1024], replicated, may hold values from 0.5 to 2
- ptdf: bfloat16 [8192, 60416], P('br', 'bus'), may hold values from -0.0234375 to 0.0234375
- branch_class: int32 [8192], P('br'), may hold values from 0 to 15
- class_limit: float32 [16], replicated, may hold values from 0.4 to 3
- class_price: float32 [16], replicated, may hold values from 0.5 to 5
Outputs:
- grad_bus: float32 [128, 60416], P('br', 'bus')
- grad_release: float32 [128, 1024], P('br')
All inputs are finite; a program needn't handle non-finite values.
Results may differ from a plain program's by a relative error of at most 0.0031.
Values may be sent and summed in bfloat16 or wider, within the bound.
A program may use at most 64 MiB of HBM per device.

v0:
```python
import jax
import jax.numpy as jnp
from jax import lax
from jax.sharding import PartitionSpec as P

SMOOTH = 0.25


def shards(net_load, release, plant_bus, efficiency, ptdf, branch_class, class_limit, class_price):
    rows_local, bus_local = net_load.shape
    offset = lax.axis_index("bus") * bus_local
    columns = plant_bus - offset
    inside = ((columns >= 0) & (columns < bus_local)).astype(jnp.float32)
    clipped = jnp.clip(columns, 0, bus_local - 1)
    weighted = efficiency * inside
    inject = (
        net_load.astype(jnp.float32)
        .at[:, clipped]
        .add(release * weighted[None, :])
        .astype(jnp.bfloat16)
    )
    partial_flows = lax.dot_general(
        lax.all_gather(inject, "br", axis=0, tiled=True),
        ptdf,
        (((1,), (1,)), ((), ())),
        preferred_element_type=jnp.float32,
    )
    onehot = (branch_class[:, None] == jnp.arange(class_limit.shape[0])[None, :]).astype(
        jnp.float32
    )
    limit = jnp.sum(onehot * class_limit[None, :], axis=1)[None, :]
    price = jnp.sum(onehot * class_price[None, :], axis=1)[None, :]
    flows = lax.psum(partial_flows, "bus")
    upper = jax.nn.sigmoid((flows - limit) / SMOOTH)
    lower = jax.nn.sigmoid((-flows - limit) / SMOOTH)
    grad_flow = (price * (upper - lower)).astype(jnp.bfloat16)
    grad_bus = lax.psum_scatter(
        jnp.dot(grad_flow, ptdf, preferred_element_type=jnp.float32),
        "br",
        scatter_dimension=0,
        tiled=True,
    )
    picked = grad_bus[:, clipped] * weighted[None, :]
    grad_release = lax.psum(picked, "bus")
    return (grad_bus, grad_release)


def solution(mesh):
    placed = (P("br", "bus"), P("br", None), P(), P(), P("br", "bus"), P("br"), P(), P())
    return jax.shard_map(
        shards,
        mesh=mesh,
        in_specs=placed,
        out_specs=(P("br", "bus"), P("br", None)),
        check_vma=False,
    )
```

profile of v0, /device:TPU:1, one launch (start us, length us, event | category | flops | bytes accessed | tf_op | source)
XLA Modules:
  0.0 980.7 jit_solution(10808538749008123875)
XLA Ops:
  7.2 0.0 all-gather.3.cloned.1.call-start
  7.2 0.7 broadcast_clamp_fusion
  7.9 0.7 and_select_fusion
  8.6 0.7 multiply_bitcast_fusion.1
  9.3 0.2 copy.25
  9.6 4.7 copy.24
  14.3 11.7 %scatter_fusion = f32[2,15104]{0,1:T(8,128)} fusion(f32[2,15104]{0,1:T(8,128)} %copy.24, s32[1024]{0:T(1024)S(1)} %get-tuple-element.13, f32[1024,2]{1,0:T(8,128)S(1)} %copy.25), kind=kCustom, calls=%fused_computation.1 | custom fusion | flops 2048 | bytes 28672 | tf_op jit(solution)/shard_map/scatter-add | solution.py:19
  26.0 4.7 convert_bitcast_fusion
  30.7 4.1 copy.26
  34.8 0.0 all-gather.3.cloned.1.call-update
  34.8 0.0 all-reduce.4.cloned.1.call-start
  34.9 126.9 %all-gather.3.cloned.1.call-done = bf16[64,2,15104]{2,1,0:T(2,128)(2,1)} async-done(((bf16[1,2,15104]{2,1,0:T(2,128)(2,1)}), bf16[64,2,15104]{2,1,0:T(2,128)(2,1)}) %all-gather.3.cloned.1.call-update) | async-done | bytes 3866640 | tf_op jit(solution)/shard_map/all_gather | solution.py:23
  161.8 8.2 reshape.29
  170.0 5.1 fusion.7
  175.1 0.0 all-reduce.4.cloned.1.call-update
  175.1 0.0 all-reduce.6.cloned.1.call-start
  175.2 0.0 copy-done.1
  175.2 0.0 copy-done.2
  175.2 0.1 select_reduce_fusion.1
  175.3 40.9 %all-reduce.4.cloned.1.call-done = f32[128,128]{1,0:T(8,128)} async-done(((f32[128,128]{1,0:T(8,128)}), f32[128,128]{1,0:T(8,128)}) %all-reduce.4.cloned.1.call-update) | async-done | bytes 65552 | tf_op jit(solution)/shard_map/psum | solution.py:33
  216.1 6.4 fusion
  222.5 0.0 all-reduce.6.cloned.1.call-update
  222.5 0.6 copy-done.4
  223.2 0.6 dynamic-slice
  224.4 681.7 %all-reduce.6.cloned.1.call-done = f32[128,15104]{1,0:T(8,128)} async-done(((f32[128,15104]{1,0:T(8,128)}), f32[128,15104]{1,0:T(8,128)}) %all-reduce.6.cloned.1.call-update) | async-done | bytes 7733264
  906.1 1.1 constant_dynamic-slice_fusion
  907.2 0.0 copy-start
  907.2 4.7 copy.27
  911.9 6.0 gather_fusion
  918.0 0.2 multiply_bitcast_fusion
  918.2 55.2 %psum.15 = f32[2,1024]{0,1:T(8,128)S(1)} all-reduce(f32[2,1024]{0,1:T(8,128)S(1)} %multiply_bitcast_fusion), channel_id=1, replica_groups=mesh['br'=64,'bus'=4] {'bus'}, use_global_device_ids=true, to_apply=%region_5.6 | all-reduce | flops 2048 | bytes 16384 | tf_op jit(solution)/shard_map/psum | solution.py:44
  973.4 0.8 copy.28
  (6 shorter events, 0.0 us)
Async XLA Ops:
  7.2 154.6 %all-gather.3.cloned.1.call-start = ((), (), s32[]{:S(2)}) async-start(), calls=%async_computation.1 | async-start | bytes 3927040 | tf_op jit(solution)/shard_map/all_gather | solution.py:23
  34.8 181.3 %all-reduce.4.cloned.1.call-start = ((), (), s32[]{:S(2)}) async-start(), calls=%async_computation | async-start | bytes 131072 | tf_op jit(solution)/shard_map/psum | solution.py:33
  170.0 5.2 copy-start.1
  170.0 5.2 copy-start.2
  170.0 5.2 copy-start.3
  175.1 731.0 %all-reduce.6.cloned.1.call-start = ((), (), s32[]{:S(2)}) async-start(), calls=%async_computation.2 | async-start | bytes 15466496
  222.5 0.7 copy-start.4
  907.2 4.7 copy-start
Sparse Core Ops, SparseCore 0:
  35.0 126.7 all-gather.2
  175.2 40.8 all-reduce.3
  222.7 683.4 all-reduce.5
where the time goes:
time: 981 us
  waiting for transfers between devices  849 us (87%)
  blocking collectives  55.2 us (6%)
  local copies, waits for them, and re-layouts  31.2 us (3%)
  other arithmetic  18.8 us (2%)
  between operations  14.5 us (1%)
  matrix products  11.5 us (1%)
    unnamed x4, waiting for transfers between devices  682 us
    all_gather x1, waiting for transfers between devices, shards(): lax.all_gather(inject, 'br', axis=0, tiled=True)  127 us
    psum x1, blocking collectives, shards(): grad_release = lax.psum(picked, 'bus')  55.2 us
    psum x1, waiting for transfers between devices, shards(): flows = lax.psum(partial_flows, 'bus')  40.9 us
  transfers between devices with their start and end apart: 3, of which 3 were waited for; matrix products, arithmetic and copies ran while one was open for 0% of the time, Pallas kernels for 0%

commit v1 on v0

--- a/solution.py
+++ b/solution.py
@@ -41,7 +41,11 @@
         tiled=True,
     )
     picked = grad_bus[:, clipped] * weighted[None, :]
-    grad_release = lax.psum(picked, "bus")
+
+    def _perform_column(mesh_dim, x0):
+        return jnp.sum(lax.all_gather(x0, mesh_dim), 0)
+
+    grad_release = _perform_column("bus", x0=picked)
     return (grad_bus, grad_release)
 
 

time: 981 us -> 972 us (level)
    psum x1 -> x0, blocking collectives: 55.2 us -> none  [shards(): grad_release = lax.psum(picked, 'bus')]
    all_gather x0 -> x1, blocking collectives: none -> 46 us  [_perform_column(): return jnp.sum(lax.all_gather(x0, mesh_dim), 0)]
where the time goes in v1:
time: 972 us
  waiting for transfers between devices  849 us (87%)
  blocking collectives  46 us (5%)
  local copies, waits for them, and re-layouts  30.6 us (3%)
  other arithmetic  19.4 us (2%)
  between operations  14.5 us (1%)
  matrix products  11.5 us (1%)
    unnamed x4, waiting for transfers between devices  682 us
    all_gather x1, waiting for transfers between devices, shards(): lax.all_gather(inject, 'br', axis=0, tiled=True)  127 us
    all_gather x1, blocking collectives, _perform_column(): return jnp.sum(lax.all_gather(x0, mesh_dim), 0)  46 us
    psum x1, waiting for transfers between devices, shards(): flows = lax.psum(partial_flows, 'bus')  40.9 us
  transfers between devices with their start and end apart: 3, of which 3 were waited for; matrix products, arithmetic and copies ran while one was open for 0% of the time, Pallas kernels for 0%

profile of v1, /device:TPU:1, one launch (start us, length us, event | category | flops | bytes accessed | tf_op | source)
XLA Modules:
  0.0 971.5 jit_solution(7856487809785804437)
XLA Ops:
  7.2 0.0 all-gather.3.cloned.1.call-start
  7.2 0.7 broadcast_clamp_fusion
  7.9 0.7 and_select_fusion
  8.6 0.7 multiply_bitcast_fusion
  9.3 0.2 copy.25
  9.6 4.7 copy.24
  14.3 11.7 %scatter_fusion = f32[2,15104]{0,1:T(8,128)} fusion(f32[2,15104]{0,1:T(8,128)} %copy.24, s32[1024]{0:T(1024)S(1)} %get-tuple-element.9, f32[1024,2]{1,0:T(8,128)S(1)} %copy.25), kind=kCustom, calls=%fused_computation.1 | custom fusion | flops 2048 | bytes 28672 | tf_op jit(solution)/shard_map/scatter-add | solution.py:19
  26.0 4.7 convert_bitcast_fusion
  30.7 4.1 copy.26
  34.8 0.0 all-gather.3.cloned.1.call-update
  34.8 0.0 all-reduce.4.cloned.1.call-start
  34.9 126.9 %all-gather.3.cloned.1.call-done = bf16[64,2,15104]{2,1,0:T(2,128)(2,1)} async-done(((bf16[1,2,15104]{2,1,0:T(2,128)(2,1)}), bf16[64,2,15104]{2,1,0:T(2,128)(2,1)}) %all-gather.3.cloned.1.call-update) | async-done | bytes 3866640 | tf_op jit(solution)/shard_map/all_gather | solution.py:23
  161.8 8.2 reshape.56
  170.0 5.1 fusion.7
  175.1 0.0 all-reduce.4.cloned.1.call-update
  175.1 0.0 all-reduce.6.cloned.1.call-start
  175.2 0.0 copy-done.1
  175.2 0.1 select_reduce_fusion.1
  175.3 40.9 %all-reduce.4.cloned.1.call-done = f32[128,128]{1,0:T(8,128)} async-done(((f32[128,128]{1,0:T(8,128)}), f32[128,128]{1,0:T(8,128)}) %all-reduce.4.cloned.1.call-update) | async-done | bytes 65552 | tf_op jit(solution)/shard_map/psum | solution.py:33
  216.1 6.4 fusion
  222.5 0.0 all-reduce.6.cloned.1.call-update
  222.5 0.6 copy-done.4
  223.2 0.6 dynamic-slice
  224.4 681.7 %all-reduce.6.cloned.1.call-done = f32[128,15104]{1,0:T(8,128)} async-done(((f32[128,15104]{1,0:T(8,128)}), f32[128,15104]{1,0:T(8,128)}) %all-reduce.6.cloned.1.call-update) | async-done | bytes 7733264
  906.1 1.1 constant_dynamic-slice_fusion
  907.2 0.0 copy-start
  907.2 4.7 copy.27
  911.9 6.0 gather_fusion
  918.0 0.2 bitcast_multiply_fusion
  918.2 0.2 copy.28
  918.3 46.0 %all_gather.8 = f32[4,2,1024]{2,1,0:T(2,128)S(1)} all-gather(f32[1,2,1024]{2,1,0:T(2,128)S(1)} %copy.28), channel_id=1, replica_groups=mesh['br'=64,'bus'=4] {'bus'}, dimensions={0}, use_global_device_ids=true | all-gather | bytes 40960 | tf_op jit(solution)/shard_map/all_gather | solution.py:46
  964.4 0.6 reduce_sum.29
  (7 shorter events, 0.0 us)
Async XLA Ops:
  7.2 154.6 %all-gather.3.cloned.1.call-start = ((), (), s32[]{:S(2)}) async-start(), calls=%async_computation.1 | async-start | bytes 3927040 | tf_op jit(solution)/shard_map/all_gather | solution.py:23
  34.8 181.3 %all-reduce.4.cloned.1.call-start = ((), (), s32[]{:S(2)}) async-start(), calls=%async_computation | async-start | bytes 131072 | tf_op jit(solution)/shard_map/psum | solution.py:33
  170.0 5.2 copy-start.1
  170.0 5.2 copy-start.2
  170.0 5.2 copy-start.3
  175.1 731.0 %all-reduce.6.cloned.1.call-start = ((), (), s32[]{:S(2)}) async-start(), calls=%async_computation.2 | async-start | bytes 15466496
  222.5 0.7 copy-start.4
  907.2 4.7 copy-start
Sparse Core Ops, SparseCore 0:
  35.0 126.7 all-gather.2
  175.2 40.8 all-reduce.3
  222.7 683.4 all-reduce.5
